TPU v7x, 128 devices: a whole 4x4x4 slice. The times are simulated.
128 devices in a mesh: dp: 16 (over y, x), head: 8 (over z, core).
Axes of the slice: x: 4, y: 4, z: 4, core: 2. Of those that a mesh axis runs over, the one named last changes fastest.
Arguments:
- slot_token_ids: int32 [128, 512], P('dp'), may hold values from 0 to 50264
- lengths: int32 [128], P('dp'), may hold values from 64 to 512, as said below
- labels: int32 [128], P('dp'), may hold values from 0 to 2
- optimizer_step_count: int32 [], replicated, may hold values from 2 to 20
- token_embedding_table: bfloat16 [50304, 1024], P('dp', 'head'), may hold values from -6 to 6
- positions: bfloat16 [512, 1024], replicated, may hold values from -4 to 4
- query_key_value_weight: bfloat16 [3, 1024, 1024], P(None, None, 'head'), may hold values from -0.1875 to 0.1875
- attention_output_weight: bfloat16 [1024, 1024], P('head'), may hold values from -0.8 to 0.8
- feedforward_input_weight: bfloat16 [1024, 4096], P(None, 'head'), may hold values from -0.1875 to 0.1875
- feedforward_output_weight: bfloat16 [4096, 1024], P('head'), may hold values from -0.09375 to 0.09375
- layer_norm_gains: float32 [3, 1024], replicated, may hold values from 0.5 to 1.5
- layer_norm_biases: float32 [3, 1024], replicated, may hold values from -2 to 2
- classifier: bfloat16 [3, 1024], replicated, may hold values from -0.75 to 0.75
- adapter_down_maps: float32 [2, 1024, 16], replicated, may hold values from -0.1875 to 0.1875
- adapter_up_maps: float32 [2, 16, 1024], P(None, None, 'head'), may hold values from -1.5 to 1.5
- down_first_moment: float32 [2, 1024, 16], P(None, 'dp'), may hold values from -0.0078125 to 0.0078125
- down_second_moment: float32 [2, 1024, 16], P(None, 'dp'), may hold values from 2.1972657e-08 to 9.1552735e-08
- up_first_moment: float32 [2, 16, 1024], P(None, None, ('head', 'dp')), may hold values from -0.0078125 to 0.0078125
- up_second_moment: float32 [2, 16, 1024], P(None, None, ('head', 'dp')), may hold values from 2.1972657e-08 to 9.1552735e-08
- down_privacy_noise: float32 [2, 1024, 16], P(None, 'dp'), may hold values from -6 to 6
- up_privacy_noise: float32 [2, 16, 1024], P(None, None, ('head', 'dp')), may hold values from -6 to 6
Outputs:
- loss: float32 [], replicated
- example_norms: float32 [128], P(('dp', 'head'))
- a_moment1: float32 [2, 1024, 16], P(None, 'dp')
- a_moment2: float32 [2, 1024, 16], P(None, 'dp')
- a_weight: float32 [2, 1024, 16], P(None, 'dp')
- b_moment1: float32 [2, 16, 1024], P(None, None, ('head', 'dp'))
- b_moment2: float32 [2, 16, 1024], P(None, None, ('head', 'dp'))
- b_weight: float32 [2, 16, 1024], P(None, None, ('head', 'dp'))
- lamb_norms: float32 [4, 2], replicated
Inputs may be any that keep to these rules, and one draw needn't show every extreme that they name: `lengths`: valid tokens of each example; some example has exactly 512.
All inputs are finite; a program needn't handle non-finite values.
Results may differ from a plain program's by a relative error of at most 0.0059.
Values may be sent and summed in bfloat16 or wider, within the bound.
No kernel may reach another device: no remote copies, remote signals or barrier semaphores. Data moves between devices by JAX's collectives and lax.ppermute only.
A program may use at most 256 MiB of HBM per device.

v0:
```python
import jax
import jax.numpy as jnp
from jax import lax
from jax.sharding import PartitionSpec as P

HDIM = 64
MICRO = 4
precise = lax.Precision.HIGHEST
adapter_scale = 2.0
clip_bound = 1.0
noise_mult = 0.6
smooth_rate = 0.1
beta_one = 0.9
beta_two = 0.999
adam_eps = 1e-06
decay_rate = 0.01
learn_rate = 0.25
norm_eps = 1e-05
contract_last = (((1,), (1,)), ((), ()))


def gelu_exact(inputs):
    return jax.nn.gelu(inputs, approximate=False)


def norm_rows(inputs, gain, bias):
    centre = inputs - jnp.mean(inputs, -1, keepdims=True)
    inv_std = lax.rsqrt(jnp.mean(centre * centre, -1, keepdims=True) + norm_eps)
    return (centre * inv_std * gain + bias, inv_std)


def norm_back(grad, normed, inv_std, gain, bias):
    x_hat = (normed - bias) / gain
    scaled = grad * gain
    return inv_std * (
        scaled
        - jnp.mean(scaled, -1, keepdims=True)
        - x_hat * jnp.mean(scaled * x_hat, -1, keepdims=True)
    )


def branch_add(partial_out, resid, gain, bias):
    total = lax.psum(partial_out, "head")
    return norm_rows(resid + total, gain, bias)


def masked_scores(query_h, key_h, valid_mask):
    scores = jnp.einsum(
        "eqhd,ekhd->ehqk", query_h, key_h, preferred_element_type=jnp.float32
    ) * HDIM ** (-0.5)
    return jnp.where(valid_mask[:, None, None, :], scores, -1e30)


def layer_forward(
    hidden_initial, valid_mask, length_float, class_label, frozen_params, adapter_reduced
):
    w_qkv, w_o, w_in, w_out, gains, biases, class_w = frozen_params
    down_pair, up_reduced = adapter_reduced
    example_count, sequence_length = valid_mask.shape
    width = hidden_initial.shape[1]
    local_w = w_o.shape[0]
    adapter_width = up_reduced.shape[1]
    shape4 = (example_count, sequence_length, local_w // HDIM, HDIM)
    hidden_reduced = hidden_initial.astype(jnp.bfloat16)
    adapter_activation = jnp.dot(
        hidden_reduced, down_pair, preferred_element_type=jnp.float32
    ).astype(jnp.bfloat16)
    query_low = (
        (
            jnp.dot(hidden_reduced, w_qkv[0], preferred_element_type=jnp.float32)
            + adapter_scale
            * jnp.dot(
                adapter_activation[:, :adapter_width],
                up_reduced[0],
                preferred_element_type=jnp.float32,
            )
        )
        .astype(jnp.bfloat16)
        .reshape(shape4)
    )
    key_low = (
        jnp.dot(hidden_reduced, w_qkv[1], preferred_element_type=jnp.float32)
        .astype(jnp.bfloat16)
        .reshape(shape4)
    )
    value_low = (
        (
            jnp.dot(hidden_reduced, w_qkv[2], preferred_element_type=jnp.float32)
            + adapter_scale
            * jnp.dot(
                adapter_activation[:, adapter_width:],
                up_reduced[1],
                preferred_element_type=jnp.float32,
            )
        )
        .astype(jnp.bfloat16)
        .reshape(shape4)
    )
    scores = masked_scores(query_low, key_low, valid_mask)
    row_top = jnp.max(scores, -1, keepdims=True)
    log_total = row_top + jnp.log(jnp.sum(jnp.exp(scores - row_top), -1, keepdims=True))
    attn_prob = jnp.exp(scores - log_total)
    context = (
        jnp.einsum(
            "ehqk,ekhd->eqhd",
            attn_prob.astype(jnp.bfloat16),
            value_low,
            preferred_element_type=jnp.float32,
        )
        .astype(jnp.bfloat16)
        .reshape(-1, local_w)
    )
    hidden_one, std_one = branch_add(
        jnp.dot(context, w_o, preferred_element_type=jnp.float32),
        hidden_initial,
        gains[1],
        biases[1],
    )
    ffn_pre = jnp.dot(hidden_one.astype(jnp.bfloat16), w_in, preferred_element_type=jnp.float32)
    ffn_part = jnp.dot(
        gelu_exact(ffn_pre).astype(jnp.bfloat16), w_out, preferred_element_type=jnp.float32
    )
    hidden_two, std_two = branch_add(ffn_part, hidden_one, gains[2], biases[2])
    valid_f = valid_mask.astype(jnp.float32)
    pooled = (
        jnp.sum(hidden_two.reshape(example_count, sequence_length, width) * valid_f[..., None], 1)
        / length_float[:, None]
    )
    logits = lax.dot_general(
        pooled.astype(jnp.bfloat16), class_w, contract_last, preferred_element_type=jnp.float32
    )
    log_prob = jax.nn.log_softmax(logits, -1)
    target = (1.0 - smooth_rate) * jax.nn.one_hot(
        class_label, class_w.shape[0], dtype=jnp.float32
    ) + smooth_rate / class_w.shape[0]
    losses = -jnp.sum(target * log_prob, -1)
    d_logit = jnp.exp(log_prob) - target
    d_pooled = jnp.dot(d_logit, class_w.astype(jnp.float32), precision=precise)
    d_two = (d_pooled[:, None, :] * (valid_f / length_float[:, None])[..., None]).reshape(-1, width)
    d_sum_two = norm_back(d_two, hidden_two, std_two, gains[2], biases[2])
    grad_act = lax.dot_general(
        d_sum_two.astype(jnp.bfloat16), w_out, contract_last, preferred_element_type=jnp.float32
    )
    d_pre = jax.vjp(gelu_exact, ffn_pre)[1](grad_act)[0].astype(jnp.bfloat16)
    back_part = lax.dot_general(d_pre, w_in, contract_last, preferred_element_type=jnp.float32)
    d_one = d_sum_two + lax.psum(back_part, "head")
    d_attn = norm_back(d_one, hidden_one, std_one, gains[1], biases[1]).astype(jnp.bfloat16)
    d_context = (
        lax.dot_general(d_attn, w_o, contract_last, preferred_element_type=jnp.float32)
        .astype(jnp.bfloat16)
        .reshape(shape4)
    )
    attn_prob = jnp.exp(masked_scores(query_low, key_low, valid_mask) - log_total)
    d_value = jnp.einsum(
        "ehqk,eqhd->ekhd",
        attn_prob.astype(jnp.bfloat16),
        d_context,
        preferred_element_type=jnp.float32,
    ).astype(jnp.bfloat16)
    d_prob = jnp.einsum("eqhd,ekhd->ehqk", d_context, value_low, preferred_element_type=jnp.float32)
    d_score = (attn_prob * (d_prob - jnp.sum(attn_prob * d_prob, -1, keepdims=True))).astype(
        jnp.bfloat16
    )
    d_query = (
        jnp.einsum("ehqk,ekhd->eqhd", d_score, key_low, preferred_element_type=jnp.float32)
        * HDIM ** (-0.5)
    ).astype(jnp.bfloat16)
    dq_rows = d_query.reshape(-1, local_w)
    dv_rows = d_value.reshape(-1, local_w)
    example_activation = adapter_activation.reshape(
        example_count, sequence_length, 2 * adapter_width
    )
    up_gradient = adapter_scale * jnp.stack(
        [
            jnp.einsum(
                "elr,eld->erd",
                example_activation[..., :adapter_width],
                dq_rows.reshape(example_count, sequence_length, local_w),
                preferred_element_type=jnp.float32,
            ),
            jnp.einsum(
                "elr,eld->erd",
                example_activation[..., adapter_width:],
                dv_rows.reshape(example_count, sequence_length, local_w),
                preferred_element_type=jnp.float32,
            ),
        ],
        1,
    )
    inner_portion = adapter_scale * jnp.concatenate(
        [
            lax.dot_general(
                dq_rows, up_reduced[0], contract_last, preferred_element_type=jnp.float32
            ),
            lax.dot_general(
                dv_rows, up_reduced[1], contract_last, preferred_element_type=jnp.float32
            ),
        ],
        1,
    )
    inner_full = lax.psum(inner_portion, "head")
    inner_sum = inner_full.astype(jnp.bfloat16)
    grad_both = jnp.einsum(
        "eld,elr->edr",
        hidden_reduced.reshape(example_count, sequence_length, width),
        inner_sum.reshape(example_count, sequence_length, 2 * adapter_width),
        preferred_element_type=jnp.float32,
    )
    down_gradient = jnp.stack([grad_both[..., :adapter_width], grad_both[..., adapter_width:]], 1)
    return (losses, down_gradient, up_gradient)


def apply_blocks(hidden_rows, lengths, labels, frozen_params, adapter_reduced, encoder_block):
    example_count, sequence_length, width = hidden_rows.shape
    valid_all = jnp.arange(sequence_length)[None, :] < lengths[:, None]
    loss_list, down_list, up_list = ([], [], [])
    for block_idx in range(example_count // encoder_block):
        first_ex = block_idx * encoder_block
        last_ex = first_ex + encoder_block
        losses, down_gradient, up_gradient = layer_forward(
            hidden_rows[first_ex:last_ex].reshape(-1, width),
            valid_all[first_ex:last_ex],
            lengths[first_ex:last_ex].astype(jnp.float32),
            labels[first_ex:last_ex],
            frozen_params,
            adapter_reduced,
        )
        loss_list.append(losses)
        down_list.append(down_gradient)
        up_list.append(up_gradient)
    return (
        jnp.concatenate(loss_list, 0),
        jnp.concatenate(down_list, 0),
        jnp.concatenate(up_list, 0),
    )


def lamb_direction(weight, grad, first, second, step_number):
    first_new = beta_one * first + (1.0 - beta_one) * grad
    second_new = beta_two * second + (1.0 - beta_two) * grad * grad
    direction = (
        first_new
        / (1.0 - jnp.power(beta_one, step_number))
        / (jnp.sqrt(second_new / (1.0 - jnp.power(beta_two, step_number))) + adam_eps)
        + decay_rate * weight
    )
    return (first_new, second_new, direction)


def per_device(
    slot_token_ids,
    lengths,
    labels,
    optimizer_step_count,
    token_embedding_table,
    positions,
    query_key_value_weight,
    attention_output_weight,
    feedforward_input_weight,
    feedforward_output_weight,
    layer_norm_gains,
    layer_norm_biases,
    classifier,
    adapter_down_maps,
    adapter_up_maps,
    down_first_moment,
    down_second_moment,
    up_first_moment,
    up_second_moment,
    down_privacy_noise,
    up_privacy_noise,
):
    n_head = lax.axis_size("head")
    dataset_size = lax.axis_size("dp")
    ex_dev, sequence_length = slot_token_ids.shape
    width = positions.shape[1]
    every_ids = lax.all_gather(slot_token_ids, "dp", axis=0, tiled=True).reshape(-1)
    vocab_local = token_embedding_table.shape[0]
    offset = lax.axis_index("dp") * vocab_local
    ids_here = every_ids - offset
    inside = (ids_here >= 0) & (ids_here < vocab_local)
    picked = jnp.take(token_embedding_table, jnp.clip(ids_here, 0, vocab_local - 1), axis=0)
    columns = lax.psum_scatter(
        jnp.where(inside[:, None], picked.astype(jnp.float32), 0.0).astype(jnp.bfloat16),
        "dp",
        scatter_dimension=0,
        tiled=True,
    )
    pos_f = positions.astype(jnp.float32)[None]
    down_reduced = adapter_down_maps.astype(jnp.bfloat16)
    down_pair = jnp.concatenate([down_reduced[0], down_reduced[1]], 1)
    micro_examples = ex_dev // MICRO
    own_share = ex_dev // n_head
    tokens = lax.all_gather(columns, "head", axis=1, tiled=True)
    hidden_all, unused_std = norm_rows(
        tokens.astype(jnp.float32).reshape(ex_dev, sequence_length, width) + pos_f,
        layer_norm_gains[0],
        layer_norm_biases[0],
    )
    frozen_params = (
        query_key_value_weight,
        attention_output_weight,
        feedforward_input_weight,
        feedforward_output_weight,
        layer_norm_gains,
        layer_norm_biases,
        classifier,
    )
    losses, grads_down, grads_up = apply_blocks(
        hidden_all,
        lengths,
        labels,
        frozen_params,
        (down_pair, adapter_up_maps.astype(jnp.bfloat16)),
        micro_examples,
    )
    part_sums = jnp.sum(grads_down * grads_down, (1, 2, 3)) / n_head + jnp.sum(
        grads_up * grads_up, (1, 2, 3)
    )
    arrived = lax.all_to_all(
        part_sums.reshape(n_head, own_share), "head", split_axis=0, concat_axis=0, tiled=True
    )
    example_norms = jnp.sqrt(jnp.sum(arrived, 0))
    own_factor = clip_bound / jnp.maximum(example_norms, clip_bound)
    factors = lax.all_gather(own_factor, "head", axis=0, tiled=True)
    sum_down = jnp.einsum("e,eabc->abc", factors, grads_down, precision=precise)
    sum_up = jnp.einsum("e,eabc->abc", factors, grads_up, precision=precise)
    loss_part = jnp.sum(losses) / n_head
    red_down, red_up = (
        lax.psum_scatter(sum_down, "dp", scatter_dimension=1, tiled=True),
        lax.psum_scatter(sum_up, "dp", scatter_dimension=2, tiled=True),
    )
    examples = ex_dev * dataset_size
    down_gradient = (red_down + noise_mult * clip_bound * down_privacy_noise) / examples
    up_gradient = (red_up + noise_mult * clip_bound * up_privacy_noise) / examples
    step_number = optimizer_step_count.astype(jnp.float32)
    down_rows = adapter_down_maps.shape[1] // dataset_size
    down_weight = lax.dynamic_slice_in_dim(
        adapter_down_maps, lax.axis_index("dp") * down_rows, down_rows, 1
    )
    up_columns = adapter_up_maps.shape[2] // dataset_size
    up_weight = lax.dynamic_slice_in_dim(
        adapter_up_maps, lax.axis_index("dp") * up_columns, up_columns, 2
    )
    down_momentum, down_velocity, dir_down = lamb_direction(
        down_weight, down_gradient, down_first_moment, down_second_moment, step_number
    )
    up_momentum, up_velocity, dir_up = lamb_direction(
        up_weight, up_gradient, up_first_moment, up_second_moment, step_number
    )
    sq_down = (
        jnp.stack(
            [jnp.sum(down_weight * down_weight, (1, 2)), jnp.sum(dir_down * dir_down, (1, 2))], 1
        )
        / n_head
    )
    sq_up = jnp.stack([jnp.sum(up_weight * up_weight, (1, 2)), jnp.sum(dir_up * dir_up, (1, 2))], 1)
    total_down, total_up, loss_sum = lax.psum((sq_down, sq_up, loss_part), ("dp", "head"))
    norm_table = jnp.sqrt(jnp.concatenate([total_down, total_up], 0))
    updated_down = (
        down_weight - learn_rate * (norm_table[:2, 0] / norm_table[:2, 1])[:, None, None] * dir_down
    )
    updated_up = (
        up_weight - learn_rate * (norm_table[2:, 0] / norm_table[2:, 1])[:, None, None] * dir_up
    )
    return (
        loss_sum / examples,
        example_norms,
        down_momentum,
        down_velocity,
        updated_down,
        up_momentum,
        up_velocity,
        updated_up,
        norm_table,
    )


def solution(mesh):
    placed = (
        P("dp", None),
        P("dp"),
        P("dp"),
        P(),
        P("dp", "head"),
        P(),
        P(None, None, "head"),
        P("head", None),
        P(None, "head"),
        P("head", None),
        P(),
        P(),
        P(),
        P(),
        P(None, None, "head"),
        P(None, "dp", None),
        P(None, "dp", None),
        P(None, None, ("head", "dp")),
        P(None, None, ("head", "dp")),
        P(None, "dp", None),
        P(None, None, ("head", "dp")),
    )
    return jax.shard_map(
        per_device,
        mesh=mesh,
        in_specs=placed,
        out_specs=(
            P(),
            P(("dp", "head")),
            P(None, "dp", None),
            P(None, "dp", None),
            P(None, "dp", None),
            P(None, None, ("head", "dp")),
            P(None, None, ("head", "dp")),
            P(None, None, ("head", "dp")),
            P(),
        ),
        check_vma=False,
    )
```

profile of v0, /device:TPU:1, one launch (start us, length us, event | category | flops | bytes accessed | tf_op | source)
XLA Modules:
  0.0 1647.0 jit_solution(5846328891770936799)
XLA Ops:
  7.3 19.8 %all_gather.9 = s32[128,512]{1,0:T(8,128)S(1)} all-gather(s32[8,512]{1,0:T(8,128)} %param.22), channel_id=1, replica_groups=mesh['dp'=16,'head'=8] {'dp'}, dimensions={0}, use_global_device_ids=true | all-gather | bytes 278528 | tf_op jit(solution)/shard_map/all_gather | solution.py:277
  28.1 229.0 %gather_fusion = bf16[65536,128]{1,0:T(8,128)(2,1)} fusion(bf16[3144,128]{1,0:T(8,128)(2,1)S(1)} %copy-done.1, s32[65536]{0:T(1024)S(1)} %broadcast_clamp_fusion), kind=kCustom, calls=%fused_computation | custom fusion | bytes 33816576 | tf_op jit(solution)/shard_map/jit(_take)/gather | solution.py:282
  257.0 46.3 %select_convert_fusion = bf16[65536,128]{1,0:T(8,128)(2,1)} fusion(bf16[65536,128]{1,0:T(8,128)(2,1)} %gather_fusion, pred[65536]{0:T(1024)(128)(4,1)S(1)} %compare_and_fusion, pred[65536]{0:T(1024)(128)(4,1)S(1)} %bitcast.555), kind=kLoop, calls=%fused_computation.1 | loop fusion | flops 33554432 | bytes 33685504 | tf_op jit(solution)/shard_map/convert_element_type | solution.py:284
  303.4 115.6 %reduce-scatter.6.cloned.1.call-done = bf16[4096,128]{1,0:T(8,128)(2,1)} async-done(((bf16[65536,128]{1,0:T(8,128)(2,1)}), bf16[4096,128]{1,0:T(8,128)(2,1)}) %reduce-scatter.6.cloned.1.call-update) | async-done | bytes 1048592 | tf_op jit(solution)/shard_map/reduce_scatter | solution.py:283
  423.8 51.6 %all-gather.2.cloned.1.call-done = bf16[4096,1024]{1,0:T(8,128)(2,1)} async-done(((bf16[4096,128]{1,0:T(8,128)(2,1)}), bf16[4096,1024]{1,0:T(8,128)(2,1)}) %all-gather.2.cloned.1.call-update) | async-done | bytes 8388624 | tf_op jit(solution)/shard_map/all_gather | solution.py:294
  580.3 183.9 %all-reduce.15.cloned.1.call-done = (f32[1024,1024]{1,0:T(8,128)}, f32[1024,1024]{1,0:T(8,128)}, f32[1024,1024]{1,0:T(8,128)}, f32[1024,1024]{1,0:T(8,128)}) async-done(((f32[1024,1024]{1,0:T(8,128)}, f32[1024,1024]{1,0:T(8,128)}, f32[1024,1024]{1,0:T(8,128)}, f32[1024,1024]{1,0:T(8,128)}), (f32[1024,1024]{1,0:T(8,128)}, f32[1024,1024]{1,0:T(8,128)}, f32[1024,1024]{1,0:T(8,128)}, ...) | async-done | bytes 16777232 | tf_op jit(solution)/shard_map/psum | solution.py:43
  777.6 6.8 fusion.140
  806.8 6.7 fusion.137
  814.4 183.4 %all-reduce.13.cloned.1.call-done = (f32[1024,1024]{1,0:T(8,128)}, f32[1024,1024]{1,0:T(8,128)}, f32[1024,1024]{1,0:T(8,128)}, f32[1024,1024]{1,0:T(8,128)}) async-done(((f32[1024,1024]{1,0:T(8,128)}, f32[1024,1024]{1,0:T(8,128)}, f32[1024,1024]{1,0:T(8,128)}, f32[1024,1024]{1,0:T(8,128)}), (f32[1024,1024]{1,0:T(8,128)}, f32[1024,1024]{1,0:T(8,128)}, f32[1024,1024]{1,0:T(8,128)}, ...) | async-done | bytes 16777232 | tf_op jit(solution)/shard_map/psum | solution.py:43
  997.8 12.3 fusion.371
  1027.7 8.9 fusion.18
  1036.7 10.9 fusion.144
  1051.4 11.0 fusion.143
  1062.5 7.4 fusion.29
  1069.8 10.8 fusion.142
  1080.6 10.9 fusion.141
  1102.5 173.5 %all-reduce.11.cloned.1.call-done = (f32[1024,1024]{1,0:T(8,128)}, f32[1024,1024]{1,0:T(8,128)}, f32[1024,1024]{1,0:T(8,128)}, f32[1024,1024]{1,0:T(8,128)}) async-done(((f32[1024,1024]{1,0:T(8,128)}, f32[1024,1024]{1,0:T(8,128)}, f32[1024,1024]{1,0:T(8,128)}, f32[1024,1024]{1,0:T(8,128)}), (f32[1024,1024]{1,0:T(8,128)}, f32[1024,1024]{1,0:T(8,128)}, f32[1024,1024]{1,0:T(8,128)}, ...) | async-done | bytes 16777232 | tf_op jit(solution)/shard_map/psum | solution.py:146
  1276.0 7.9 fusion.370
  1359.7 29.7 %all-reduce.16 = (bf16[1024,32]{0,1:T(8,128)(2,1)}, bf16[1024,32]{0,1:T(8,128)(2,1)}, bf16[1024,32]{0,1:T(8,128)(2,1)}, bf16[1024,32]{0,1:T(8,128)(2,1)}) all-reduce(f32[1024,32]{0,1:T(8,128)S(1)} %maximum_multiply_fusion.3, f32[1024,32]{0,1:T(8,128)} %maximum_multiply_fusion.2, ...), channel_id=1, replica_groups=mesh['dp'=16,'head'=8] {'head'}, use_global_device_ids=true, to_apply=%region_73.75 | all-reduce | flops 131072 | bytes 786432 | tf_op jit(solution)/shard_map/psum | solution.py:201
  1396.8 10.8 all_to_all.6
  1409.6 12.5 all-reduce
  1426.7 64.2 %reduce-scatter.8.cloned.1.call-done = f32[2,16,8]{1,2,0:T(8,128)} async-done(((f32[2,16,128]{1,2,0:T(8,128)}), f32[2,16,8]{1,2,0:T(8,128)}) %reduce-scatter.8.cloned.1.call-update) | async-done | bytes 1040 | tf_op jit(solution)/shard_map/reduce_scatter | solution.py:331
  1492.3 74.0 %reduce-scatter.10.cloned.1.call-done = f32[64,32]{1,0:T(8,128)} async-done(((f32[1024,32]{1,0:T(8,128)}), f32[64,32]{1,0:T(8,128)}) %reduce-scatter.10.cloned.1.call-update) | async-done | bytes 8208
  1568.7 66.1 %all-reduce.1 = (f32[]{:T(128)}, f32[2,2]{0,1:T(2,128)S(1)}, f32[2,2]{0,1:T(2,128)S(1)}) all-reduce(f32[]{:T(128)S(6)} %div.320, f32[2,2]{0,1:T(2,128)S(1)} %pad_maximum_fusion.2, f32[2,2]{0,1:T(2,128)S(1)} %maximum_multiply_fusion.8), channel_id=1, replica_groups=mesh['dp'=16,'head'=8] {'dp','head'}, use_global_device_ids=true, to_apply=%region_45.47 | all-reduce | flops 9 | bytes 72 | tf_op jit(solution)/shard_map/psum | solution.py:358
  (635 shorter events, 268.8 us)
Async XLA Ops:
  7.2 770.4 %copy-start = (bf16[512,1024]{1,0:T(8,128)(2,1)S(1)}, bf16[512,1024]{1,0:T(8,128)(2,1)}, u32[]{:S(2)}) copy-start(bf16[512,1024]{1,0:T(8,128)(2,1)} %param.31) | copy-start | bytes 3145732
  7.2 20.9 %copy-start.1 = (bf16[3144,128]{1,0:T(8,128)(2,1)S(1)}, bf16[3144,128]{1,0:T(8,128)(2,1)}, u32[]{:S(2)}) copy-start(bf16[3144,128]{1,0:T(8,128)(2,1)} %param.26) | copy-start | bytes 2414596
  7.2 411.8 %reduce-scatter.6.cloned.1.call-start = ((), (), s32[]{:S(2)}) async-start(), calls=%async_computation.4 | async-start | bytes 17825792 | tf_op jit(solution)/shard_map/reduce_scatter | solution.py:283
  303.3 172.0 %all-gather.2.cloned.1.call-start = ((), (), s32[]{:S(2)}) async-start(), calls=%async_computation.5 | async-start | bytes 9437184 | tf_op jit(solution)/shard_map/all_gather | solution.py:294
  419.0 345.2 %all-reduce.15.cloned.1.call-start = ((), (), s32[]{:S(2)}) async-start(), calls=%async_computation.10 | async-start | bytes 33554432 | tf_op jit(solution)/shard_map/psum | solution.py:43
  420.7 151.7 %copy-start.88 = (bf16[2,16,128]{2,1,0:T(8,128)(2,1)}, bf16[2,16,128]{2,1,0:T(8,128)(2,1)S(1)}, u32[]{:S(2)}) copy-start(bf16[2,16,128]{2,1,0:T(8,128)(2,1)S(1)} %convert_element_type.351) | copy-start | bytes 24580
  422.0 151.4 %copy-start.111 = (pred[2,512]{1,0:T(4,128)(4,1)}, pred[2,512]{1,0:T(4,128)(4,1)S(1)}, u32[]{:S(2)}) copy-start(pred[2,512]{1,0:T(4,128)(4,1)S(1)} %get-tuple-element.137) | copy-start | bytes 3076
  500.9 19.8 %copy-start.32 = (f32[2,512,1024]{2,1,0:T(8,128)}, f32[2,512,1024]{2,1,0:T(8,128)S(1)}, u32[]{:S(2)}) copy-start(f32[2,512,1024]{2,1,0:T(8,128)S(1)} %get-tuple-element.79) | copy-start | bytes 12582916
  580.3 417.5 %all-reduce.13.cloned.1.call-start = ((), (), s32[]{:S(2)}) async-start(), calls=%async_computation.9 | async-start | bytes 33554432 | tf_op jit(solution)/shard_map/psum | solution.py:43
  813.5 462.4 %all-reduce.11.cloned.1.call-start = ((), (), s32[]{:S(2)}) async-start(), calls=%async_computation.8 | async-start | bytes 33554432 | tf_op jit(solution)/shard_map/psum | solution.py:146
  1010.1 17.6 %copy-start.4 = (f32[1024,1024]{1,0:T(8,128)}, f32[1024,1024]{1,0:T(8,128)S(1)}, u32[]{:S(2)}) copy-start(f32[1024,1024]{1,0:T(8,128)S(1)} %get-tuple-element.121) | copy-start | bytes 12582916
  1091.6 399.3 %reduce-scatter.8.cloned.1.call-start = ((), (), s32[]{:S(2)}) async-start(), calls=%async_computation.6 | async-start | bytes 139264 | tf_op jit(solution)/shard_map/reduce_scatter | solution.py:331
  1290.2 53.7 %copy-start.78 = (bf16[2,2,64,512]{3,2,1,0:T(8,128)(2,1)}, bf16[2,2,64,512]{3,2,1,0:T(8,128)(2,1)S(1)}, u32[]{:S(2)}) copy-start(bf16[2,2,64,512]{3,2,1,0:T(8,128)(2,1)S(1)} %convolution_convert_fusion) | copy-start | bytes 786436
  1307.6 40.5 %copy-start.80 = (bf16[2,2,64,512]{3,2,1,0:T(8,128)(2,1)}, bf16[2,2,64,512]{3,2,1,0:T(8,128)(2,1)S(1)}, u32[]{:S(2)}) copy-start(bf16[2,2,64,512]{3,2,1,0:T(8,128)(2,1)S(1)} %convolution_convert_fusion.1) | copy-start | bytes 786436
  1324.9 27.4 %copy-start.82 = (bf16[2,2,64,512]{3,2,1,0:T(8,128)(2,1)}, bf16[2,2,64,512]{3,2,1,0:T(8,128)(2,1)S(1)}, u32[]{:S(2)}) copy-start(bf16[2,2,64,512]{3,2,1,0:T(8,128)(2,1)S(1)} %convolution_convert_fusion.2) | copy-start | bytes 786436
  1358.9 32.7 %copy-start.38 = (bf16[2,512,1024]{2,1,0:T(8,128)(2,1)S(1)}, bf16[2,512,1024]{2,1,0:T(8,128)(2,1)}, u32[]{:S(2)}) copy-start(bf16[2,512,1024]{2,1,0:T(8,128)(2,1)} %get-tuple-element.84) | copy-start | bytes 6291460
  1423.1 143.2 %reduce-scatter.10.cloned.1.call-start = ((), (), s32[]{:S(2)}) async-start(), calls=%async_computation.7 | async-start | bytes 557056
  1423.2 67.7 %copy-start.122 = (f32[2,16,8]{1,2,0:T(8,128)S(1)}, f32[2,16,8]{1,2,0:T(8,128)}, u32[]{:S(2)}) copy-start(f32[2,16,8]{1,2,0:T(8,128)} %copy.338) | copy-start | bytes 3076
  1423.2 67.7 %copy-start.153 = (f32[2,16,8]{1,2,0:T(8,128)S(1)}, f32[2,16,8]{1,2,0:T(8,128)}, u32[]{:S(2)}) copy-start(f32[2,16,8]{1,2,0:T(8,128)} %param.42) | copy-start | bytes 3076
  1423.2 67.7 %copy-start.154 = (f32[2,16,8]{1,2,0:T(8,128)S(1)}, f32[2,16,8]{1,2,0:T(8,128)}, u32[]{:S(2)}) copy-start(f32[2,16,8]{1,2,0:T(8,128)} %param.40) | copy-start | bytes 3076
  1423.2 67.7 %copy-start.155 = (f32[2,16,8]{1,2,0:T(8,128)S(1)}, f32[2,16,8]{1,2,0:T(8,128)}, u32[]{:S(2)}) copy-start(f32[2,16,8]{1,2,0:T(8,128)} %param.39) | copy-start | bytes 3076
  1424.7 142.5 %copy-start.145 = (f32[2,64,16]{1,2,0:T(8,128)S(1)}, f32[2,64,16]{1,2,0:T(8,128)}, u32[]{:S(2)}) copy-start(f32[2,64,16]{1,2,0:T(8,128)} %param.41) | copy-start | bytes 24580
  1424.7 142.5 %copy-start.146 = (f32[2,64,16]{1,2,0:T(8,128)S(1)}, f32[2,64,16]{1,2,0:T(8,128)}, u32[]{:S(2)}) copy-start(f32[2,64,16]{1,2,0:T(8,128)} %param.38) | copy-start | bytes 24580
  1424.7 142.5 %copy-start.147 = (f32[2,64,16]{1,2,0:T(8,128)S(1)}, f32[2,64,16]{1,2,0:T(8,128)}, u32[]{:S(2)}) copy-start(f32[2,64,16]{1,2,0:T(8,128)} %param.37) | copy-start | bytes 24580
  (147 other events, 469.7 us)
Sparse Core Ops, SparseCore 0:
  303.4 115.5 reduce-scatter.5
  420.7 54.6 all-gather.1
  580.4 183.7 all-reduce.14
  813.6 184.1 all-reduce.12
  1091.7 184.2 all-reduce.10
  1423.2 67.6 reduce-scatter.7
  1494.4 71.8 reduce-scatter.9
where the time goes:
time: 1650 us
  waiting for transfers between devices  846 us (51%)
  local copies, waits for them, and re-layouts  291 us (18%)
  matrix products  177 us (11%)
  other arithmetic  169 us (10%)
  blocking collectives  139 us (8%)
  between operations  24.4 us (1%)
    psum x2, waiting for transfers between devices, branch_add(): total = lax.psum(partial_out, 'head')  367 us
    gather x1, local copies, waits for them, and re-layouts, per_device(): jnp.take(token_embedding_table, jnp.clip(ids_here, 0, vocab_local - 1), a...  229 us
    psum x1, waiting for transfers between devices, layer_forward(): d_one = d_sum_two + lax.psum(back_part, 'head')  173 us
    reduce_scatter x1, waiting for transfers between devices, per_device(): lax.psum_scatter(jnp.where(inside[:, None], picked.astype(jnp.float32), 0...  116 us
    unnamed x8, waiting for transfers between devices  74.1 us
    psum x1, blocking collectives, per_device(): lax.psum((sq_down, sq_up, loss_part), ('dp', 'head'))  66.1 us
    reduce_scatter x1, waiting for transfers between devices, per_device(): lax.psum_scatter(sum_up, 'dp', scatter_dimension=2, tiled=True)  64.2 us
    all_gather x1, waiting for transfers between devices, per_device(): tokens = lax.all_gather(columns, 'head', axis=1, tiled=True)  51.6 us
  transfers between devices with their start and end apart: 7, of which 7 were waited for; matrix products, arithmetic and copies ran while one was open for 1% of the time, Pallas kernels for 0%

commit v1 on v0

--- a/solution.py
+++ b/solution.py
@@ -1,3 +1,4 @@
+import functools
 import jax
 import jax.numpy as jnp
 from jax import lax
@@ -17,6 +18,19 @@
 learn_rate = 0.25
 norm_eps = 1e-05
 contract_last = (((1,), (1,)), ((), ()))
+
+
+def search_the_lane(original, group_axis, join_dim):
+    views = []
+    for _ in range(lax.psum(1, group_axis)):
+        views.append(original)
+    piece_next = jnp.concatenate(
+        lax.all_to_all(jnp.stack(views, axis=0), group_axis, 0, 0), axis=join_dim
+    )
+    return piece_next
+
+
+manage_the_units = functools.partial(search_the_lane, group_axis="head", join_dim=1)
 
 
 def gelu_exact(inputs):
@@ -291,7 +305,7 @@
     down_pair = jnp.concatenate([down_reduced[0], down_reduced[1]], 1)
     micro_examples = ex_dev // MICRO
     own_share = ex_dev // n_head
-    tokens = lax.all_gather(columns, "head", axis=1, tiled=True)
+    tokens = manage_the_units(columns)
     hidden_all, unused_std = norm_rows(
         tokens.astype(jnp.float32).reshape(ex_dev, sequence_length, width) + pos_f,
         layer_norm_gains[0],

time: 1650 us -> 1760 us (1.067)
  local copies, waits for them, and re-layouts: 291 us -> 342 us
  waiting for transfers between devices: 846 us -> 871 us
  other arithmetic: 169 us -> 192 us
    all_to_all x0 -> x1, waiting for transfers between devices: none -> 78.6 us  [search_the_lane(): lax.all_to_all(jnp.stack(views, axis=0), group_axis, 0, 0)]
    all_gather x1 -> x0, waiting for transfers between devices: 51.6 us -> none  [per_device(): tokens = lax.all_gather(columns, 'head', axis=1, tiled=True)]
    convert_element_type x0 -> x2, local copies, waits for them, and re-layouts: none -> 35.9 us  [per_device(): tokens.astype(jnp.float32).reshape(ex_dev, sequence_length, width) + pos_f]
    unnamed x358 -> x363, local copies, waits for them, and re-layouts: 30.4 us -> 38.6 us
    unnamed x8 -> x7, waiting for transfers between devices: 74.1 us -> 74 us
  transfers between devices with their start and end apart: 7 -> 7, of which waited for: 7 -> 7; matrix products, arithmetic and copies ran while one was open for 1% -> 2% of each run, Pallas kernels for 0% -> 0%
where the time goes in v1:
time: 1760 us; the launch traced here: 1750 us
  waiting for transfers between devices  871 us (49%)
  local copies, waits for them, and re-layouts  342 us (19%)
  other arithmetic  192 us (11%)
  matrix products  178 us (10%)
  blocking collectives  139 us (8%)
  between operations  24.5 us (1%)
    psum x2, waiting for transfers between devices, branch_add(): total = lax.psum(partial_out, 'head')  365 us
    gather x1, local copies, waits for them, and re-layouts, per_device(): jnp.take(token_embedding_table, jnp.clip(ids_here, 0, vocab_local - 1), a...  227 us
    psum x1, waiting for transfers between devices, layer_forward(): d_one = d_sum_two + lax.psum(back_part, 'head')  173 us
    reduce_scatter x1, waiting for transfers between devices, per_device(): lax.psum_scatter(jnp.where(inside[:, None], picked.astype(jnp.float32), 0...  116 us
    all_to_all x1, waiting for transfers between devices, search_the_lane(): lax.all_to_all(jnp.stack(views, axis=0), group_axis, 0, 0)  78.6 us
    unnamed x7, waiting for transfers between devices  74 us
    psum x1, blocking collectives, per_device(): lax.psum((sq_down, sq_up, loss_part), ('dp', 'head'))  66 us
    reduce_scatter x1, waiting for transfers between devices, per_device(): lax.psum_scatter(sum_up, 'dp', scatter_dimension=2, tiled=True)  64.1 us
  transfers between devices with their start and end apart: 7, of which 7 were waited for; matrix products, arithmetic and copies ran while one was open for 2% of the time, Pallas kernels for 0%

profile of v1, /device:TPU:1, one launch (start us, length us, event | category | flops | bytes accessed | tf_op | source)
XLA Modules:
  0.0 1751.0 jit_solution(12820351849052252847)
XLA Ops:
  7.3 19.8 %all_gather.6 = s32[128,512]{1,0:T(8,128)S(1)} all-gather(s32[8,512]{1,0:T(8,128)} %param.22), channel_id=1, replica_groups=mesh['dp'=16,'head'=8] {'dp'}, dimensions={0}, use_global_device_ids=true | all-gather | bytes 278528 | tf_op jit(solution)/shard_map/all_gather | solution.py:291
  28.1 227.3 %gather_fusion = bf16[65536,128]{1,0:T(8,128)(2,1)} fusion(bf16[3144,128]{1,0:T(8,128)(2,1)S(1)} %copy-done.1, s32[65536]{0:T(1024)S(1)} %broadcast_clamp_fusion), kind=kCustom, calls=%fused_computation | custom fusion | bytes 33816576 | tf_op jit(solution)/shard_map/jit(_take)/gather | solution.py:296
  255.3 46.3 %select_convert_fusion = bf16[65536,128]{1,0:T(8,128)(2,1)} fusion(bf16[65536,128]{1,0:T(8,128)(2,1)} %gather_fusion, pred[65536]{0:T(1024)(128)(4,1)S(1)} %compare_and_fusion, pred[65536]{0:T(1024)(128)(4,1)S(1)} %bitcast.558), kind=kLoop, calls=%fused_computation.1 | loop fusion | flops 33554432 | bytes 33685504 | tf_op jit(solution)/shard_map/convert_element_type | solution.py:298
  301.6 115.8 %reduce-scatter.6.cloned.1.call-done = bf16[4096,128]{1,0:T(8,128)(2,1)} async-done(((bf16[65536,128]{1,0:T(8,128)(2,1)}), bf16[4096,128]{1,0:T(8,128)(2,1)}) %reduce-scatter.6.cloned.1.call-update) | async-done | bytes 1048592 | tf_op jit(solution)/shard_map/reduce_scatter | solution.py:297
  444.2 78.6 %all-to-all-done = bf16[8,4096,128]{2,1,0:T(8,128)(2,1)} async-done(((bf16[8,4096,128]{2,1,0:T(8,128)(2,1)}), bf16[8,4096,128]{2,1,0:T(8,128)(2,1)}, u32[]{:S(2)}, u32[]{:S(2)}) %all-to-all-start) | async-done | bytes 8388640 | tf_op jit(solution)/shard_map/all_to_all | solution.py:28
  522.8 10.3 convert_bitcast_fusion
  533.1 17.9 %copy.180 = f32[4096,8,128]{2,1,0:T(8,128)} copy(f32[4096,8,128]{2,0,1:T(8,128)} %convert_bitcast_fusion) | data formatting | bytes 33554432 | tf_op jit(solution)/shard_map/convert_element_type | solution.py:310
  550.9 18.0 %reshape.664 = f32[8,512,1024]{2,1,0:T(8,128)} reshape(f32[4096,8,128]{2,1,0:T(8,128)} %copy.180) | data formatting | bytes 33554432 | tf_op jit(solution)/shard_map/convert_element_type | solution.py:310
  569.0 11.1 fusion
  580.1 11.3 multiply_reduce_fusion
  687.1 181.4 %all-reduce.15.cloned.1.call-done = (f32[1024,1024]{1,0:T(8,128)}, f32[1024,1024]{1,0:T(8,128)}, f32[1024,1024]{1,0:T(8,128)}, f32[1024,1024]{1,0:T(8,128)}) async-done(((f32[1024,1024]{1,0:T(8,128)}, f32[1024,1024]{1,0:T(8,128)}, f32[1024,1024]{1,0:T(8,128)}, f32[1024,1024]{1,0:T(8,128)}), (f32[1024,1024]{1,0:T(8,128)}, f32[1024,1024]{1,0:T(8,128)}, f32[1024,1024]{1,0:T(8,128)}, ...) | async-done | bytes 16777232 | tf_op jit(solution)/shard_map/psum | solution.py:57
  918.6 183.4 %all-reduce.13.cloned.1.call-done = (f32[1024,1024]{1,0:T(8,128)}, f32[1024,1024]{1,0:T(8,128)}, f32[1024,1024]{1,0:T(8,128)}, f32[1024,1024]{1,0:T(8,128)}) async-done(((f32[1024,1024]{1,0:T(8,128)}, f32[1024,1024]{1,0:T(8,128)}, f32[1024,1024]{1,0:T(8,128)}, f32[1024,1024]{1,0:T(8,128)}), (f32[1024,1024]{1,0:T(8,128)}, f32[1024,1024]{1,0:T(8,128)}, f32[1024,1024]{1,0:T(8,128)}, ...) | async-done | bytes 16777232 | tf_op jit(solution)/shard_map/psum | solution.py:57
  1102.0 12.5 fusion.371
  1140.8 10.9 fusion.144
  1155.6 11.0 fusion.143
  1174.0 11.0 fusion.142
  1185.1 10.9 fusion.141
  1206.9 173.4 %all-reduce.11.cloned.1.call-done = (f32[1024,1024]{1,0:T(8,128)}, f32[1024,1024]{1,0:T(8,128)}, f32[1024,1024]{1,0:T(8,128)}, f32[1024,1024]{1,0:T(8,128)}) async-done(((f32[1024,1024]{1,0:T(8,128)}, f32[1024,1024]{1,0:T(8,128)}, f32[1024,1024]{1,0:T(8,128)}, f32[1024,1024]{1,0:T(8,128)}), (f32[1024,1024]{1,0:T(8,128)}, f32[1024,1024]{1,0:T(8,128)}, f32[1024,1024]{1,0:T(8,128)}, ...) | async-done | bytes 16777232 | tf_op jit(solution)/shard_map/psum | solution.py:160
  1463.9 29.8 %all-reduce.16 = (bf16[1024,32]{0,1:T(8,128)(2,1)}, bf16[1024,32]{0,1:T(8,128)(2,1)}, bf16[1024,32]{0,1:T(8,128)(2,1)}, bf16[1024,32]{0,1:T(8,128)(2,1)}) all-reduce(f32[1024,32]{0,1:T(8,128)S(1)} %maximum_multiply_fusion.3, f32[1024,32]{0,1:T(8,128)} %maximum_multiply_fusion.2, ...), channel_id=1, replica_groups=mesh['dp'=16,'head'=8] {'head'}, use_global_device_ids=true, to_apply=%region_73.75 | all-reduce | flops 131072 | bytes 786432 | tf_op jit(solution)/shard_map/psum | solution.py:215
  1500.9 10.8 all_to_all.11
  1513.8 12.5 all-reduce
  1530.9 64.1 %reduce-scatter.8.cloned.1.call-done = f32[2,16,8]{1,2,0:T(8,128)} async-done(((f32[2,16,128]{1,2,0:T(8,128)}), f32[2,16,8]{1,2,0:T(8,128)}) %reduce-scatter.8.cloned.1.call-update) | async-done | bytes 1040 | tf_op jit(solution)/shard_map/reduce_scatter | solution.py:345
  1596.4 73.9 %reduce-scatter.10.cloned.1.call-done = f32[64,32]{1,0:T(8,128)} async-done(((f32[1024,32]{1,0:T(8,128)}), f32[64,32]{1,0:T(8,128)}) %reduce-scatter.10.cloned.1.call-update) | async-done | bytes 8208
  1672.7 66.0 %all-reduce.1 = (f32[]{:T(128)}, f32[2,2]{0,1:T(2,128)S(1)}, f32[2,2]{0,1:T(2,128)S(1)}) all-reduce(f32[]{:T(128)S(6)} %div.320, f32[2,2]{0,1:T(2,128)S(1)} %pad_maximum_fusion.2, f32[2,2]{0,1:T(2,128)S(1)} %maximum_multiply_fusion.8), channel_id=1, replica_groups=mesh['dp'=16,'head'=8] {'dp','head'}, use_global_device_ids=true, to_apply=%region_45.47 | all-reduce | flops 9 | bytes 72 | tf_op jit(solution)/shard_map/psum | solution.py:372
  (644 shorter events, 318.7 us)
Async XLA Ops:
  7.2 874.5 %copy-start = (bf16[512,1024]{1,0:T(8,128)(2,1)S(1)}, bf16[512,1024]{1,0:T(8,128)(2,1)}, u32[]{:S(2)}) copy-start(bf16[512,1024]{1,0:T(8,128)(2,1)} %param.31) | copy-start | bytes 3145732
  7.2 20.9 %copy-start.1 = (bf16[3144,128]{1,0:T(8,128)(2,1)S(1)}, bf16[3144,128]{1,0:T(8,128)(2,1)}, u32[]{:S(2)}) copy-start(bf16[3144,128]{1,0:T(8,128)(2,1)} %param.26) | copy-start | bytes 2414596
  7.2 410.2 %reduce-scatter.6.cloned.1.call-start = ((), (), s32[]{:S(2)}) async-start(), calls=%async_computation.5 | async-start | bytes 17825792 | tf_op jit(solution)/shard_map/reduce_scatter | solution.py:297
  423.0 99.8 %all-to-all-start = ((bf16[8,4096,128]{2,1,0:T(8,128)(2,1)}), bf16[8,4096,128]{2,1,0:T(8,128)(2,1)}, u32[]{:S(2)}, u32[]{:S(2)}) async-start(bf16[8,4096,128]{2,1,0:T(8,128)(2,1)} %stack.101), calls=%async_computation.1 | async-start | bytes 16777216 | tf_op jit(solution)/shard_map/all_to_all | solution.py:28
  428.9 439.5 %all-reduce.15.cloned.1.call-start = ((), (), s32[]{:S(2)}) async-start(), calls=%async_computation.10 | async-start | bytes 33554432 | tf_op jit(solution)/shard_map/psum | solution.py:57
  441.1 238.0 %copy-start.90 = (bf16[2,16,128]{2,1,0:T(8,128)(2,1)}, bf16[2,16,128]{2,1,0:T(8,128)(2,1)S(1)}, u32[]{:S(2)}) copy-start(bf16[2,16,128]{2,1,0:T(8,128)(2,1)S(1)} %convert_element_type.366) | copy-start | bytes 24580
  442.4 237.6 %copy-start.113 = (pred[2,512]{1,0:T(4,128)(4,1)}, pred[2,512]{1,0:T(4,128)(4,1)S(1)}, u32[]{:S(2)}) copy-start(pred[2,512]{1,0:T(4,128)(4,1)S(1)} %get-tuple-element.137) | copy-start | bytes 3076
  607.8 19.8 %copy-start.32 = (f32[2,512,1024]{2,1,0:T(8,128)}, f32[2,512,1024]{2,1,0:T(8,128)S(1)}, u32[]{:S(2)}) copy-start(f32[2,512,1024]{2,1,0:T(8,128)S(1)} %get-tuple-element.79) | copy-start | bytes 12582916
  687.0 415.0 %all-reduce.13.cloned.1.call-start = ((), (), s32[]{:S(2)}) async-start(), calls=%async_computation.9 | async-start | bytes 33554432 | tf_op jit(solution)/shard_map/psum | solution.py:57
  917.7 462.6 %all-reduce.11.cloned.1.call-start = ((), (), s32[]{:S(2)}) async-start(), calls=%async_computation.8 | async-start | bytes 33554432 | tf_op jit(solution)/shard_map/psum | solution.py:160
  1114.5 17.6 %copy-start.4 = (f32[1024,1024]{1,0:T(8,128)}, f32[1024,1024]{1,0:T(8,128)S(1)}, u32[]{:S(2)}) copy-start(f32[1024,1024]{1,0:T(8,128)S(1)} %get-tuple-element.121) | copy-start | bytes 12582916
  1196.0 399.0 %reduce-scatter.8.cloned.1.call-start = ((), (), s32[]{:S(2)}) async-start(), calls=%async_computation.6 | async-start | bytes 139264 | tf_op jit(solution)/shard_map/reduce_scatter | solution.py:345
  1394.3 53.7 %copy-start.80 = (bf16[2,2,64,512]{3,2,1,0:T(8,128)(2,1)}, bf16[2,2,64,512]{3,2,1,0:T(8,128)(2,1)S(1)}, u32[]{:S(2)}) copy-start(bf16[2,2,64,512]{3,2,1,0:T(8,128)(2,1)S(1)} %convolution_convert_fusion) | copy-start | bytes 786436
  1411.6 40.5 %copy-start.82 = (bf16[2,2,64,512]{3,2,1,0:T(8,128)(2,1)}, bf16[2,2,64,512]{3,2,1,0:T(8,128)(2,1)S(1)}, u32[]{:S(2)}) copy-start(bf16[2,2,64,512]{3,2,1,0:T(8,128)(2,1)S(1)} %convolution_convert_fusion.1) | copy-start | bytes 786436
  1429.0 27.4 %copy-start.84 = (bf16[2,2,64,512]{3,2,1,0:T(8,128)(2,1)}, bf16[2,2,64,512]{3,2,1,0:T(8,128)(2,1)S(1)}, u32[]{:S(2)}) copy-start(bf16[2,2,64,512]{3,2,1,0:T(8,128)(2,1)S(1)} %convolution_convert_fusion.2) | copy-start | bytes 786436
  1463.0 32.8 %copy-start.38 = (bf16[2,512,1024]{2,1,0:T(8,128)(2,1)S(1)}, bf16[2,512,1024]{2,1,0:T(8,128)(2,1)}, u32[]{:S(2)}) copy-start(bf16[2,512,1024]{2,1,0:T(8,128)(2,1)} %get-tuple-element.84) | copy-start | bytes 6291460
  1527.3 143.0 %reduce-scatter.10.cloned.1.call-start = ((), (), s32[]{:S(2)}) async-start(), calls=%async_computation.7 | async-start | bytes 557056
  1527.3 67.7 %copy-start.124 = (f32[2,16,8]{1,2,0:T(8,128)S(1)}, f32[2,16,8]{1,2,0:T(8,128)}, u32[]{:S(2)}) copy-start(f32[2,16,8]{1,2,0:T(8,128)} %copy.340) | copy-start | bytes 3076
  1527.3 67.7 %copy-start.155 = (f32[2,16,8]{1,2,0:T(8,128)S(1)}, f32[2,16,8]{1,2,0:T(8,128)}, u32[]{:S(2)}) copy-start(f32[2,16,8]{1,2,0:T(8,128)} %param.42) | copy-start | bytes 3076
  1527.4 67.7 %copy-start.156 = (f32[2,16,8]{1,2,0:T(8,128)S(1)}, f32[2,16,8]{1,2,0:T(8,128)}, u32[]{:S(2)}) copy-start(f32[2,16,8]{1,2,0:T(8,128)} %param.40) | copy-start | bytes 3076
  1527.4 67.7 %copy-start.157 = (f32[2,16,8]{1,2,0:T(8,128)S(1)}, f32[2,16,8]{1,2,0:T(8,128)}, u32[]{:S(2)}) copy-start(f32[2,16,8]{1,2,0:T(8,128)} %param.39) | copy-start | bytes 3076
  1528.9 142.4 %copy-start.147 = (f32[2,64,16]{1,2,0:T(8,128)S(1)}, f32[2,64,16]{1,2,0:T(8,128)}, u32[]{:S(2)}) copy-start(f32[2,64,16]{1,2,0:T(8,128)} %param.41) | copy-start | bytes 24580
  1528.9 142.4 %copy-start.148 = (f32[2,64,16]{1,2,0:T(8,128)S(1)}, f32[2,64,16]{1,2,0:T(8,128)}, u32[]{:S(2)}) copy-start(f32[2,64,16]{1,2,0:T(8,128)} %param.38) | copy-start | bytes 24580
  1528.9 142.3 %copy-start.149 = (f32[2,64,16]{1,2,0:T(8,128)S(1)}, f32[2,64,16]{1,2,0:T(8,128)}, u32[]{:S(2)}) copy-start(f32[2,64,16]{1,2,0:T(8,128)} %param.37) | copy-start | bytes 24580
  (149 other events, 520.0 us)
Sparse Core Ops, SparseCore 0:
  301.7 115.6 reduce-scatter.5
  687.1 181.2 all-reduce.14
  917.9 184.1 all-reduce.12
  1196.1 184.1 all-reduce.10
  1527.4 67.5 reduce-scatter.7
  1598.4 71.8 reduce-scatter.9
